TPU v7x, 256 devices: a whole 4x4x8 slice. The times are simulated.
256 devices in a mesh: gx: 32 (over x_hi, z, core), gy: 8 (over x_lo, y).
Axes of the slice: x: 4 (x_hi: 2, x_lo: 2; x = x_hi * 2 + x_lo), y: 4, z: 8, core: 2. Of those that a mesh axis runs over, the one named last changes fastest.
Arguments:
- positions: float32 [3, 131072], P(None, ('gx', 'gy')), as said below
- species: int32 [131072], P(('gx', 'gy')), may hold values from 0 to 7
- send_lists: int32 [32, 8, 8, 32], P('gx', 'gy'), may hold values from 0 to 511, as said below
- cell_pairs: int32 [32, 8, 32, 2], P('gx', 'gy'), may hold values from 0 to 23, as said below
- block_count: int32 [32, 8], P('gx', 'gy'), may hold values from 24 to 32, as said below
- embed: float32 [8, 128], replicated, may hold values from -6 to 6
- radial_one: float32 [2, 8, 128], replicated, may hold values from -2 to 2
- mix_one: float32 [5, 128, 128], replicated, may hold values from -0.5 to 0.5
- radial_two: float32 [2, 8, 128], replicated, may hold values from -2 to 2
- mix_two: float32 [2, 128, 128], replicated, may hold values from -0.5 to 0.5
- readout: float32 [2, 128], replicated, may hold values from -0.5 to 0.5
Outputs:
- forces: float32 [3, 131072], P(None, ('gx', 'gy'))
- site_energy: float32 [131072], P(('gx', 'gy'))
Inputs may be any that keep to these rules, and one draw needn't show every extreme that they name: `positions`: every coordinate lies in 0 to 5120^(1/3) in its owner's frame. `send_lists`: each entry names 32 distinct atoms of the sending device, as indices 0 to 511 among its own atoms. `cell_pairs`: column 0 is an owned cell 0 to 15, column 1 a cell 0 to 23 of the extended table; the first 24 slots of a device name every extended cell once in column 1. `block_count`: the number of used leading slots of each device; some device uses all 32 and some only 24.
All inputs are finite; a program needn't handle non-finite values.
Results may differ from a plain program's by a relative error of at most 0.0003.
Values sent between devices are 32-bit elements; how exact they have to be, the bound alone decides.
No kernel may reach another device: no remote copies, remote signals or barrier semaphores. Data moves between devices by JAX's collectives and lax.ppermute only.
A program may use at most 64 MiB of HBM per device.

v0:
```python
import functools

import jax
import jax.numpy as jnp
import numpy as np
from jax import lax
from jax.experimental import pallas as pl
from jax.experimental.pallas import tpu as pltpu
from jax.sharding import PartitionSpec as P

NB = 8
CELL = 32
CH = 128
LANES = 128
OWN = 16
CUT2 = 25.0
STEPS_X = np.array([-1, -1, -1, 0, 0, 1, 1, 1])
STEPS_Y = np.array([-1, 0, 1, -1, 1, -1, 0, 1])
F32 = jnp.float32
BF16 = jnp.bfloat16
VMEM = pltpu.VMEM
SMEM = pltpu.SMEM
HBM = pltpu.HBM
PARAMS = pltpu.CompilerParams(vmem_limit_bytes=20 * 1024 * 1024)
CHUNK = 128
HIST = 256
FEAT = 512
SLOTS = 32
UNROLL_OWN = (8, 4)
EARLY = 8
UNROLL_GHOST = (8, 2)
UP = (2, 4, 7)
DOWN = (0, 3, 5)
MID = (1, 6)

NN = (((1,), (0,)), ((), ()))
NT = (((1,), (1,)), ((), ()))
TN = (((0,), (0,)), ((), ()))


def split(x):
    hi = x.astype(BF16)
    return hi, (x - hi.astype(F32)).astype(BF16)


def mm(a, b, dims):
    return lax.dot_general(a, b, dims, preferred_element_type=F32)


def mm3(a, b, dims):
    (ah, al), (bh, bl) = a, b
    return mm(ah, bh, dims) + (mm(ah, bl, dims) + mm(al, bh, dims))


def mm3_deep(a, b, dims):
    (ah, al), (bh, bl) = a, b
    axis = dims[0][1][0]
    return mm(jnp.concatenate([ah, al], axis=1), jnp.concatenate([bh, bh], axis=axis), dims) + mm(ah, bl, dims)


def mm3_wide(a, b, dims):
    (ah, al), (bh, bl) = a, b
    width = 128
    out = mm(ah, jnp.concatenate([bh, bl], axis=1 - dims[0][1][0]), dims)
    return out[:, :width] + (out[:, width:] + mm(al, bh, dims))


def mm3_full(a, b, dims):
    (ah, al), (bh, bl) = a, b
    axis = dims[0][1][0]
    top = jnp.concatenate([bh, bh], axis=axis)
    low = jnp.concatenate([bl, jnp.zeros_like(bl)], axis=axis)
    out = mm(jnp.concatenate([ah, al], axis=1), jnp.concatenate([top, low], axis=1 - axis), dims)
    return out[:, :128] + out[:, 128:]


def iota(shape, dim):
    return lax.broadcasted_iota(jnp.int32, shape, dim)


def cell_rows(c):
    return pl.ds(pl.multiple_of(c * CELL, CELL), CELL)


def chunk_rows(i):
    return pl.ds(pl.multiple_of(i * CHUNK, CHUNK), CHUNK)


def geometry(r, c, keep, prc, xt):
    own = prc[cell_rows(r), :]
    far = xt[c]
    vec = [far[t + 1 : t + 2, :] - own[:, t : t + 1] for t in range(3)]
    sq = vec[0] * vec[0] + vec[1] * vec[1] + vec[2] * vec[2]
    group = iota((CELL, LANES), 1) // CELL
    edge = jnp.maximum(1.0 - sq * (1.0 / CUT2), 0.0)
    slope = edge * keep
    vk = jnp.where(group == 0, 1.0, jnp.where(group == 1, vec[0], jnp.where(group == 2, vec[1], vec[2])))
    scaled = sq * ((NB - 1) / CUT2)
    return edge * slope, slope, scaled, vk


def own_keep(r, c, weight):
    lane = iota((CELL, LANES), 1)
    row = iota((CELL, LANES), 0)
    return jnp.where(jnp.logical_and(lane % CELL == row, r == c), 0.0, weight)


def basis(scaled, n):
    off = scaled - float(n)
    return jnp.exp(-(off * off))


def all_bases(scaled):
    return [basis(scaled, n) for n in range(NB)]


def pair_force(deriv, bases, env, slope, scaled, vk):
    total = None
    moment = None
    for n in range(NB):
        term = deriv[n] * bases[n]
        total = term if n == 0 else total + term
        if n == 1:
            moment = term
        elif n > 1:
            moment = moment + float(n) * term
    spacing = CUT2 / (NB - 1)
    by_sq = (-2.0 / CUT2) * slope * total - (2.0 / spacing) * env * (scaled * total - moment)
    by_sq = by_sq * vk
    by_sq = by_sq + pltpu.roll(by_sq, 64, 1)
    by_sq = by_sq + pltpu.roll(by_sq, 32, 1)
    return env * total + 2.0 * vk * by_sq


def add_force(force, r, c, recv, send):
    recv[cell_rows(r), :] += force
    send[pl.ds(c, 1), :] += jnp.sum(force, axis=0, keepdims=True)


def species_tile(c, xt):
    row = iota((4 * NB, LANES), 0)
    lane = iota((4 * NB, LANES), 1)
    kind = xt[c][0:1, :].astype(jnp.int32)
    hit = jnp.logical_and(kind == row % NB, lane // CELL == row // NB)
    hot = jnp.where(hit, 1.0, 0.0).astype(BF16)
    zero = jnp.zeros_like(hot)
    return jnp.concatenate(
        [jnp.concatenate([hot if j == k else zero for k in range(4)], axis=1) for j in range(4)], axis=0
    )


def add_histogram(r, c, keep, prc, xt, hist, tiles, shapes, slot):
    env, slope, scaled, vk = geometry(r, c, keep, prc, xt)
    bases = all_bases(scaled)
    m = env * vk
    parts = [split(m * e) for e in bases]
    tiles[slot] = jnp.concatenate([jnp.concatenate([p[k] for p in parts], axis=0) for k in range(2)], axis=1)
    shapes[slot] = jnp.concatenate(bases + [env, slope, scaled, vk], axis=0)
    wide = [
        jnp.concatenate([p[k] for p in parts[4 * h : 4 * h + 4]], axis=1) for k in range(2) for h in range(2)
    ]
    out = mm(jnp.concatenate(wide, axis=0), species_tile(c, xt), NT)
    out = out[: 2 * CELL] + out[2 * CELL :]
    hist[cell_rows(r), :] += jnp.concatenate([out[:CELL], out[CELL:]], axis=1)


def first_deriv(r, c, xt, quad):
    q = quad[cell_rows(r), :]
    q = jnp.concatenate([q[:, :LANES], q[:, LANES:]], axis=0)
    out = mm(jnp.concatenate(split(q), axis=0), species_tile(c, xt), NN)
    out = out[: 2 * CELL] + out[2 * CELL :]
    return [out[(n // 4) * CELL : (n // 4 + 1) * CELL, (n % 4) * LANES : (n % 4 + 1) * LANES] for n in range(NB)]


def cell_features(table, c):
    hi, lo = split(table[cell_rows(c), :])
    zero = jnp.zeros((CELL, CH), BF16)

    def lay(x):
        rows = [jnp.concatenate([x[:, :CH], zero], axis=1)]
        rows += [jnp.concatenate([zero, x[:, (t + 1) * CH : (t + 2) * CH]], axis=1) for t in range(3)]
        return jnp.concatenate(rows, axis=0)

    return lay(hi), lay(lo)


def spread(g, radial):
    both = [
        jnp.concatenate([g * radial[0, n : n + 1, :], g * radial[1, n : n + 1, :]], axis=1) for n in range(NB)
    ]
    return split(jnp.concatenate(both, axis=0))


def add_forward(r, c, tile, table, radial, acc):
    fh, fl = cell_features(table, c)
    prod = mm(tile, jnp.concatenate([fh, fh], axis=0), NN) + mm(tile[:, :LANES], fl, NN)
    part = None
    for n in range(NB):
        rows = prod[n * CELL : (n + 1) * CELL]
        term = rows[:, :CH] * radial[0, n : n + 1, :] + rows[:, CH:] * radial[1, n : n + 1, :]
        part = term if n == 0 else part + term
    acc[cell_rows(r), :] += part


def add_feature_grad(r, c, tile, grad_acc, radial, grad_table):
    uh, ul = spread(grad_acc[cell_rows(r), :], radial)
    gf = mm(tile, uh, TN)
    gf = gf[:LANES] + (gf[LANES:] + mm(tile[:, :LANES], ul, TN))
    grad_table[cell_rows(c), :] += jnp.concatenate(
        [gf[0:CELL, :CH]] + [gf[(t + 1) * CELL : (t + 2) * CELL, CH:] for t in range(3)], axis=1
    )


def second_deriv(r, c, grad_acc, radial, table):
    out = mm3_wide(spread(grad_acc[cell_rows(r), :], radial), cell_features(table, c), NT)
    return [out[n * CELL : (n + 1) * CELL] for n in range(NB)]


def for_blocks(plan, unroll, body, skip=0):
    count = plan[2 * SLOTS]
    large, small = unroll
    whole = (count - skip) // large
    start = skip + whole * large

    def step(first, size):
        def run(i, carry):
            for k in range(size):
                slot = first + i * size + k
                weight = jnp.where(slot < count, 1.0, 0.0).astype(F32)
                body(plan[2 * slot], plan[2 * slot + 1], weight, slot)
            return carry

        return run

    lax.fori_loop(0, whole, step(skip, large), 0)
    lax.fori_loop(0, (count - start + small - 1) // small, step(start, small), 0)


def species_weights(embed, radial):
    zero = jnp.zeros((NB, CH), F32)
    rows = []
    for n in range(NB):
        for k in range(4):
            part = embed * radial[min(k, 1), n : n + 1, :]
            rows.append(jnp.concatenate([part if j == k else zero for j in range(4)], axis=1))
    return split(jnp.concatenate(rows, axis=0))


def tile_group(x, k):
    x = jnp.where(iota(x.shape, 1) // CELL == k, x, 0.0)
    x = x + pltpu.roll(x, 64, 1)
    return x + pltpu.roll(x, 32, 1)


def store_pieces(pieces, up, down, mid):
    for out, order in ((up, UP), (down, DOWN), (mid, MID)):
        size = pieces[0].shape[0]
        for k, p in enumerate(order):
            out[k * size : (k + 1) * size, :] = pieces[p]


def arrived(left, right, up, down, size):
    at = lambda x, k: x[k * size : (k + 1) * size, :]
    return [at(right, 0), at(right, 1), at(right, 2), at(up, 1), at(down, 1), at(left, 0), at(left, 1), at(left, 2)]


def fetch(sems, *pairs):
    copies = [pltpu.make_async_copy(src, dst, sems.at[k]) for k, (src, dst) in enumerate(pairs)]
    for copy in copies:
        copy.start()
    return copies


def arrive(copies):
    for copy in copies:
        copy.wait()


def pack_kernel(pos_in, species_in, lists_in, up, down, mid, table_out, row_out, pos, species, lists, sems):
    arrive(fetch(sems, (pos_in, pos), (species_in, species), (lists_in, lists)))
    kinds = species[...].astype(F32)
    table = jnp.concatenate([kinds, pos[...], jnp.zeros((4, kinds.shape[1]), F32)], axis=0)
    table_out[...] = table
    hi = table.astype(BF16)
    rest = table - hi.astype(F32)
    mid_part = rest.astype(BF16)
    low = (rest - mid_part.astype(F32)).astype(BF16)
    row = jnp.concatenate([lists[p : p + 1, :] for p in range(8)], axis=1)
    row_out[...] = row.astype(F32)
    hot = jnp.where(iota((table.shape[1], row.shape[1]), 0) == row, 1.0, 0.0).astype(BF16)
    out = mm(hi, hot, NN) + mm(mid_part, hot, NN) + mm(low, hot, NN)
    pieces = [
        jnp.concatenate([out[k : k + 1, p * CELL : (p + 1) * CELL] for k in range(4)], axis=1) for p in range(8)
    ]
    store_pieces(pieces, up, down, mid)


def weight_kernel(
    count, table, row, pairs_in, embed_in, radial_one_in, mix_one_in, radial_two_in, mix_two_in, readout_in,
    w_hi, w_lo, mats, begins, radial, rows, xt, prc, hot, hot_t, plan_own, plan_ghost,
    pairs, embed, radial_one, mix_one, radial_two, mix_two, readout, sems,
):
    sources = (pairs_in, embed_in, radial_one_in, mix_one_in, radial_two_in, mix_two_in, readout_in)
    targets = (pairs, embed, radial_one, mix_one, radial_two, mix_two, readout)
    copies = fetch(sems, *zip(sources, targets))
    lists = row[...].astype(jnp.int32)
    hot[...] = jnp.where(iota(hot.shape, 0) == lists, 1.0, 0.0).astype(BF16)
    column = jnp.broadcast_to(row[...], (8, row.shape[1])).T[:, 0:1].astype(jnp.int32)
    hot_t[...] = jnp.where(iota(hot_t.shape, 1) == column, 1.0, 0.0).astype(BF16)
    t = table[...]
    for c in range(OWN):
        xt[c] = tile_group(t[:, (c // 4) * LANES : (c // 4 + 1) * LANES], c % 4)
    prc[...] = jnp.concatenate([t[1:4], t[0:1], t[4:8]], axis=0).T
    arrive(copies[:1])
    def clear(i, carry):
        plan_own[i] = 0
        plan_ghost[i] = 0
        return carry

    lax.fori_loop(0, 2 * SLOTS, clear, 0)

    def sort(i, carry):
        n_own, n_ghost = carry
        r, c = pairs[0, i], pairs[1, i]
        mine = c < OWN

        @pl.when(mine)
        def _():
            plan_own[2 * n_own] = r
            plan_own[2 * n_own + 1] = c

        @pl.when(jnp.logical_not(mine))
        def _():
            plan_ghost[2 * n_ghost] = r
            plan_ghost[2 * n_ghost + 1] = c - OWN

        step = mine.astype(jnp.int32)
        return n_own + step, n_ghost + 1 - step

    n_own, n_ghost = lax.fori_loop(0, count[0, 0], sort, (jnp.int32(0), jnp.int32(0)))
    plan_own[2 * SLOTS] = n_own
    plan_ghost[2 * SLOTS] = n_ghost
    arrive(copies[1:])
    w_hi[...], w_lo[...] = species_weights(embed[...], 0.5 * radial_one[...])
    for k, m in enumerate((mix_one[0], mix_one[4], mix_one[1], mix_one[3], mix_two[0])):
        mats[0, k * CH : (k + 1) * CH, :], mats[1, k * CH : (k + 1) * CH, :] = split(m)
    begins[0], begins[1] = split(mm3(split(embed[...]), split(mix_one[2]), NT))
    radial[...] = 0.5 * radial_two[...]
    both = readout[...]
    rows[0:1, :] = both[0:1, :] + mm3(split(both), split(mix_two[1]), NN)[1:2, :]
    rows[1:2, :] = both[1:2, :]


def own_first_kernel(plan_own, xt, prc, hist, tiles, shapes):
    hist[...] = jnp.zeros_like(hist)

    def block(r, c, weight, slot):
        add_histogram(r, c, own_keep(r, c, weight), prc, xt, hist, tiles, shapes, slot)

    for_blocks(plan_own, UNROLL_OWN, block)


def ghost_first_kernel(
    side, plan, hot_t, left, right, up, down, prc, hist_own,
    hist, xt, tiles, shapes, send_up, send_down, send_mid,
):
    rows = jnp.concatenate(arrived(left, right, up, down, 1), axis=0)
    for k in range(4):
        part = tile_group(rows, k)
        for p in range(8):
            shift = 0.0 if k in (0, 3) else float((STEPS_X, STEPS_Y)[k - 1][p] * side)
            xt[p, k : k + 1, :] = part[p : p + 1, :] + shift
    hist[...] = hist_own[...]

    def block(r, c, weight, slot):
        add_histogram(r, c, weight, prc, xt, hist, tiles, shapes, slot)

    for_blocks(plan, UNROLL_GHOST, block)

    hi, lo = split(hist[...])
    sent = mm(hot_t[...], hi, NN) + mm(hot_t[...], lo, NN)
    store_pieces([sent[p * CELL : (p + 1) * CELL] for p in range(8)], send_up, send_down, send_mid)


def first_update(joined, kind, weights, begin, mix04, mix1, mix3):
    size = joined.shape[0]
    a = mm3(split(joined), weights, NN)
    a0 = a[:, :CH]
    a1 = [a[:, (t + 1) * CH : (t + 2) * CH] for t in range(3)]
    power = a1[0] * a1[0] + a1[1] * a1[1] + a1[2] * a1[2]
    both = mm3_deep(split(a0), mix04, NT)
    z0 = both[:, :CH] + mm3_full(split(power), mix1, NT)
    gate = jax.nn.sigmoid(both[:, CH:])
    hot = jnp.where(kind == iota((size, NB), 1), 1.0, 0.0).astype(BF16)
    own = mm(hot, begin[0], NN) + mm(hot, begin[1], NN)
    lift = mm3_full(split(jnp.concatenate(a1, axis=0)), mix3, NT)
    lift = jnp.concatenate([lift[t * size : (t + 1) * size] for t in range(3)], axis=1)
    feat = jnp.concatenate(
        [z0 * jax.nn.sigmoid(z0) + own, lift * jnp.concatenate([gate] * 3, axis=1)], axis=1
    )
    return feat, a, jnp.concatenate([z0, gate], axis=1), lift


def first_pullback(gs, gv, a, gates, lift, weights, mix04, mix1, mix3):
    size = gs.shape[0]
    z0, gate = gates[:, :CH], gates[:, CH:]
    sg = jax.nn.sigmoid(z0)
    dz0 = gs * (sg * (1.0 + z0 * (1.0 - sg)))
    y = [lift[:, t * CH : (t + 1) * CH] for t in range(3)]
    dgate = gv[0] * y[0] + gv[1] * y[1] + gv[2] * y[2]
    dz4 = dgate * gate * (1.0 - gate)
    da0 = mm3_wide(split(jnp.concatenate([dz0, dz4], axis=1)), mix04, NN)
    dpower = 2.0 * mm3_full(split(dz0), mix1, NN)
    dy = mm3_full(split(jnp.concatenate([v * gate for v in gv], axis=0)), mix3, NN)
    parts = [da0] + [
        dy[t * size : (t + 1) * size] + a[:, (t + 1) * CH : (t + 2) * CH] * dpower for t in range(3)
    ]
    return mm3(split(jnp.concatenate(parts, axis=1)), weights, NT)


def mat(mats, first, rows):
    return mats[0, first : first + rows, :], mats[1, first : first + rows, :]


def mixes(mats):
    return mat(mats, 0, 2 * CH), mat(mats, 2 * CH, CH), mat(mats, 3 * CH, CH)


def features(g):
    return g[:, :CH], [g[:, (t + 1) * CH : (t + 2) * CH] for t in range(3)]


def own_update_kernel(joined, prc, w_hi, w_lo, begins, mats, feat, acc, gates, lifted):
    begin = begins[0], begins[1]
    mix_all = mixes(mats)

    def chunk(i, carry):
        rows = chunk_rows(i)
        kind = prc[rows, :][:, 3:4].astype(jnp.int32)
        out = first_update(joined[rows, :], kind, (w_hi[...], w_lo[...]), begin, *mix_all)
        feat[rows, :], acc[rows, :], gates[rows, :], lifted[rows, :] = out
        return carry

    lax.fori_loop(0, feat.shape[0] // CHUNK, chunk, 0)


def own_second_kernel(plan, tiles, feat, radial, acc):
    acc[...] = jnp.zeros_like(acc)

    def block(r, c, weight, slot):
        add_forward(r, c, tiles[slot], feat, radial, acc)

    for_blocks(plan, UNROLL_OWN, block)


def ghost_second_kernel(
    plan, tiles, xt, left, right, up, down, w_hi, w_lo, begins, mats, acc_own, radial, readout,
    zed, grad_acc, feat, send_up, send_down, send_mid,
    joined, lin, gates, lifted, grad_table, acc,
):
    ghosts = feat.shape[0]
    for p, piece in enumerate(arrived(left, right, up, down, CELL)):
        joined[p * CELL : (p + 1) * CELL, :] = piece
    begin = begins[0], begins[1]
    mix_all = mixes(mats)
    acc[...] = acc_own[...]
    grad_table[...] = jnp.zeros_like(grad_table)
    kinds = jnp.concatenate([xt[p][0:8, 0:CELL] for p in range(8)], axis=1).T[:, 0:1].astype(jnp.int32)
    for i in range(ghosts // CHUNK):
        rows = pl.ds(i * CHUNK, CHUNK)
        kind = kinds[i * CHUNK : (i + 1) * CHUNK]
        out = first_update(joined[rows, :], kind, (w_hi[...], w_lo[...]), begin, *mix_all)
        feat[rows, :], lin[rows, :], gates[rows, :], lifted[rows, :] = out

    def forward(r, c, weight, slot):
        add_forward(r, c, tiles[slot], feat, radial, acc)

    for_blocks(plan, UNROLL_GHOST, forward)

    mix0 = mat(mats, 4 * CH, CH)

    def chunk(i, carry):
        rows = chunk_rows(i)
        z = mm3_full(split(acc[rows, :]), mix0, NT)
        zed[rows, :] = z
        sg = jax.nn.sigmoid(z)
        gz = readout[1:2, :] * (sg * (1.0 + z * (1.0 - sg)))
        grad_acc[rows, :] = mm3_full(split(gz), mix0, NN)
        return carry

    lax.fori_loop(0, acc.shape[0] // CHUNK, chunk, 0)

    def backward(r, c, weight, slot):
        add_feature_grad(r, c, tiles[slot], grad_acc, radial, grad_table)

    for_blocks(plan, UNROLL_GHOST, backward)

    pieces = []
    for i in range(ghosts // CHUNK):
        rows = pl.ds(i * CHUNK, CHUNK)
        gs, gv = features(grad_table[rows, :])
        q = first_pullback(gs, gv, lin[rows, :], gates[rows, :], lifted[rows, :], (w_hi[...], w_lo[...]), *mix_all)
        pieces += [q[k * CELL : (k + 1) * CELL] for k in range(CHUNK // CELL)]
    store_pieces(pieces, send_up, send_down, send_mid)


def own_grad_kernel(
    plan, tiles, grad_acc, radial, lin, gates, lifted, w_hi, w_lo, mats, readout,
    quad,
    grad_table,
):
    atoms = quad.shape[0]
    grad_table[...] = jnp.zeros_like(grad_table)

    def block(r, c, weight, slot):
        add_feature_grad(r, c, tiles[slot], grad_acc, radial, grad_table)

    for_blocks(plan, UNROLL_OWN, block)
    mix_all = mixes(mats)
    carry_w = readout[0:1, :]

    def chunk(i, carry):
        rows = chunk_rows(i)
        gs, gv = features(grad_table[rows, :])
        quad[rows, :] = first_pullback(
            gs + carry_w, gv, lin[rows, :], gates[rows, :], lifted[rows, :], (w_hi[...], w_lo[...]), *mix_all
        )
        return carry

    lax.fori_loop(0, atoms // CHUNK, chunk, 0)


def shape_of(shapes, slot):
    whole = shapes[slot]
    parts = [whole[k * CELL : (k + 1) * CELL] for k in range(12)]
    return [parts[:NB]] + parts[NB:]


def ghost_force_kernel(plan, shapes, grad_acc, radial, feat, recv, send):
    recv[...] = jnp.zeros_like(recv)
    send[...] = jnp.zeros_like(send)

    def block(r, c, weight, slot):
        deriv = second_deriv(r, c, grad_acc, radial, feat)
        add_force(pair_force(deriv, *shape_of(shapes, slot)), r, c, recv, send)

    for_blocks(plan, UNROLL_GHOST, block)


def ghost_last_kernel(
    plan, hot, shapes, xt, quad_own, left, right, up, down, recv_two, send_two,
    quad, recv, send_up, send_down, send_mid,
    back_hi, back_lo, send,
):
    for p, piece in enumerate(arrived(left, right, up, down, CELL)):
        hi, lo = split(piece)
        back_hi[p * CELL : (p + 1) * CELL, :] = hi
        back_lo[p * CELL : (p + 1) * CELL, :] = lo
    recv[...] = recv_two[...]
    send[...] = send_two[...]

    def chunk(i, carry):
        rows = chunk_rows(i)
        pick = hot[rows, :]
        quad[rows, :] = quad_own[rows, :] + (mm(pick, back_hi[...], NN) + mm(pick, back_lo[...], NN))
        return carry

    lax.fori_loop(0, quad.shape[0] // CHUNK, chunk, 0)

    def block(r, c, weight, slot):
        add_force(pair_force(first_deriv(r, c, xt, quad), *shape_of(shapes, slot)), r, c, recv, send)

    for_blocks(plan, UNROLL_GHOST, block)
    store_pieces([send[p : p + 1, :] for p in range(8)], send_up, send_down, send_mid)


def by_axis(rows, count):
    lines = [
        jnp.concatenate([rows[p : p + 1, (t + 1) * CELL : (t + 2) * CELL] for p in range(count)], axis=1)
        for t in range(3)
    ]
    return lines


def add_own_force(plan, slot, shapes, xt, quad, grad_acc, radial, feat, recv, send):
    r, c = plan[2 * slot], plan[2 * slot + 1]
    one = first_deriv(r, c, xt, quad)
    two = second_deriv(r, c, grad_acc, radial, feat)
    add_force(pair_force([x + y for x, y in zip(one, two)], *shape_of(shapes, slot)), r, c, recv, send)


def own_start_kernel(
    plan, shapes, xt, quad, grad_acc, radial, feat, recv_ghost, zed, readout, recv, send, energy
):
    recv[...] = recv_ghost[...]
    send[...] = jnp.zeros_like(send)
    z = zed[...]
    site = readout[0:1, :] * feat[:, :CH] + readout[1:2, :] * (z * jax.nn.sigmoid(z))
    hi, lo = split(site)
    ones = jnp.ones((8, CH), BF16)
    energy[...] = (mm(ones, hi, NT) + mm(ones, lo, NT))[0:1, :]
    for slot in range(EARLY):
        add_own_force(plan, slot, shapes, xt, quad, grad_acc, radial, feat, recv, send)


def own_force_kernel(
    plan, shapes, xt, quad, grad_acc, radial, feat, recv_start, send_start, out, recv, send
):
    recv[...] = recv_start[...]
    send[...] = send_start[...]

    def block(r, c, weight, slot):
        add_own_force(plan, slot, shapes, xt, quad, grad_acc, radial, feat, recv, send)

    for_blocks(plan, UNROLL_OWN, block, EARLY)
    pick = jnp.where(iota((8, LANES), 0) + 1 == iota((8, LANES), 1) // CELL, 1.0, 0.0).astype(BF16)
    hi, lo = split(recv[...])
    total = mm(pick, hi, NT) + mm(pick, lo, NT)
    out[...] = total[0:3, :] - jnp.concatenate(by_axis(send, OWN), axis=0)


def last_kernel(hot, left, right, up, down, partial, out):
    rows = jnp.concatenate(arrived(left, right, up, down, 1), axis=0)
    lines = by_axis(rows, 8)
    back = jnp.concatenate(lines + [jnp.zeros((5, lines[0].shape[1]), F32)], axis=0)
    hi, lo = split(back)
    ghost = mm(hi, hot[...], NT) + mm(lo, hot[...], NT)
    out[...] = partial[...] - ghost[0:3, :]


def ring(axis, step):
    count = lax.axis_size(axis)
    return [(i, (i + step) % count) for i in range(count)]


def swap_both(axis, to_lower, to_upper):
    count = lax.axis_size(axis)
    even = lax.axis_index(axis) % 2 == 0
    inner = [(i, i ^ 1) for i in range(count)]
    outer = [(i, (i - 1) % count if i % 2 == 0 else (i + 1) % count) for i in range(count)]
    one = lax.ppermute(jnp.where(even, to_upper, to_lower), axis, inner)
    two = lax.ppermute(jnp.where(even, to_lower, to_upper), axis, outer)
    return jnp.where(even, one, two), jnp.where(even, two, one)


def exchange(up, down, mid, between=None):
    size = mid.shape[0] // 2
    part = lambda x, k: x[k * size : (k + 1) * size]
    down, up = swap_both("gy", down, up)
    if between is not None:
        up, down, between = lax.optimization_barrier((up, down, between))
    to_left = jnp.concatenate([part(up, 0), part(mid, 0), part(down, 0)])
    to_right = jnp.concatenate([part(up, 2), part(mid, 1), part(down, 2)])
    left, right = swap_both("gx", to_left, to_right)
    return (left, right, up, down), between


def in_hbm(*arrays):
    return [pltpu.with_memory_space_constraint(x, HBM) for x in arrays]


def call(kernel, outs, specs, scratch=()):
    spaces = [SMEM if s[1] == jnp.int32 else VMEM for s in outs]
    return pl.pallas_call(
        kernel,
        out_shape=[jax.ShapeDtypeStruct(*s) for s in outs],
        in_specs=[pl.BlockSpec(memory_space=s) for s in specs],
        out_specs=[pl.BlockSpec(memory_space=s) for s in spaces],
        scratch_shapes=list(scratch),
        compiler_params=PARAMS,
    )


def shards(
    positions, species, send_lists, cell_pairs, block_count,
    embed, radial_one, mix_one, radial_two, mix_two, readout,
):
    atoms = positions.shape[1]
    side = float((atoms * 10.0) ** (1.0 / 3.0))
    pairs = cell_pairs[0, 0].T
    lists = send_lists[0, 0]
    kinds = species[None, :]
    ghosts = lists.size
    f = lambda *shape: (shape, F32)
    b = lambda *shape: (shape, BF16)
    i = lambda *shape: (shape, jnp.int32)
    three = lambda size, width: [f(3 * size, width), f(3 * size, width), f(2 * size, width)]

    *sends, table, row = call(
        pack_kernel,
        three(1, LANES) + [f(8, atoms), f(1, ghosts)],
        [HBM] * 3,
        [
            VMEM((3, atoms), F32),
            VMEM((1, atoms), jnp.int32),
            VMEM((8, CELL), jnp.int32),
            pltpu.SemaphoreType.DMA((3,)),
        ],
    )(*in_hbm(positions, kinds, lists))
    ready = call(
        weight_kernel,
        [
            b(HIST, FEAT), b(HIST, FEAT), b(2, 5 * CH, CH), b(2, NB, CH), f(2, NB, CH), f(2, CH),
            f(OWN, 8, LANES), f(atoms, 8), b(atoms, ghosts), b(ghosts, atoms),
            i(2 * SLOTS + 1), i(2 * SLOTS + 1),
        ],
        [SMEM] + [VMEM] * 2 + [HBM] * 7,
        [SMEM(pairs.shape, jnp.int32)]
        + [VMEM(x.shape, F32) for x in (embed, radial_one, mix_one, radial_two, mix_two, readout)]
        + [pltpu.SemaphoreType.DMA((7,))],
    )(block_count, table, row, *in_hbm(pairs, embed, radial_one, mix_one, radial_two, mix_two, readout))
    moved, ready = exchange(*sends, ready)
    w_hi, w_lo, mats, begins, radial, rows, xt_own, prc, hot, hot_t, plan_own, plan_ghost = ready
    store = lambda slots: [b(slots, HIST, 2 * LANES), f(slots, 12 * CELL, LANES)]
    hist_own, tiles_own, shapes_own = call(
        own_first_kernel, [f(atoms, HIST)] + store(SLOTS), [SMEM] + [VMEM] * 2
    )(plan_own, xt_own, prc)
    hist, xt_ghost, tiles_ghost, shapes_ghost, *sends = call(
        functools.partial(ghost_first_kernel, side),
        [f(atoms, HIST), f(8, 8, LANES)] + store(SLOTS // 2) + three(CELL, HIST),
        [SMEM] + [VMEM] * 7,
    )(plan_ghost, hot_t, *moved, prc, hist_own)

    own = call(
        own_update_kernel, [f(atoms, FEAT), f(atoms, FEAT), f(atoms, 2 * CH), f(atoms, 3 * CH)], [VMEM] * 6
    )(hist, prc, w_hi, w_lo, begins, mats)
    moved, own = exchange(*sends, own)
    feat, lin, gates, lifted = own
    (acc_own,) = call(own_second_kernel, [f(atoms, CH)], [SMEM] + [VMEM] * 3)(plan_own, tiles_own, feat, radial)
    zed, grad_acc, feat_ghost, *sends = call(
        ghost_second_kernel,
        [f(atoms, CH), f(atoms, CH), f(ghosts, FEAT)] + three(CELL, HIST),
        [SMEM] + [VMEM] * 13,
        [
            VMEM((ghosts, HIST), F32),
            VMEM((ghosts, FEAT), F32),
            VMEM((ghosts, 2 * CH), F32),
            VMEM((ghosts, 3 * CH), F32),
            VMEM((ghosts, FEAT), F32),
            VMEM((atoms, CH), F32),
        ],
    )(plan_ghost, tiles_ghost, xt_ghost, *moved, w_hi, w_lo, begins, mats, acc_own, radial, rows)

    two = call(ghost_force_kernel, [f(atoms, LANES), f(8, LANES)], [SMEM] + [VMEM] * 4)(
        plan_ghost, shapes_ghost, grad_acc, radial, feat_ghost
    )
    moved, two = exchange(*sends, two)
    recv_two, send_two = two
    (quad_own,) = call(
        own_grad_kernel, [f(atoms, HIST)], [SMEM] + [VMEM] * 10, [VMEM((atoms, FEAT), F32)]
    )(plan_own, tiles_own, grad_acc, radial, lin, gates, lifted, w_hi, w_lo, mats, rows)
    quad, recv, *sends = call(
        ghost_last_kernel,
        [f(atoms, HIST), f(atoms, LANES)] + three(1, LANES),
        [SMEM] + [VMEM] * 10,
        [VMEM((ghosts, HIST), BF16), VMEM((ghosts, HIST), BF16), VMEM((8, LANES), F32)],
    )(plan_ghost, hot, shapes_ghost, xt_ghost, quad_own, *moved, recv_two, send_two)

    shared = (plan_own, shapes_own, xt_own, quad, grad_acc, radial, feat)
    early = call(
        own_start_kernel, [f(atoms, LANES), f(OWN, LANES), f(1, atoms)], [SMEM] + [VMEM] * 9
    )(*shared, recv, zed, rows)
    moved, early = exchange(*sends, early)
    recv, send, energy = early
    (partial,) = call(
        own_force_kernel,
        [f(3, atoms)],
        [SMEM] + [VMEM] * 8,
        [VMEM((atoms, LANES), F32), VMEM((OWN, LANES), F32)],
    )(*shared, recv, send)
    (forces,) = call(last_kernel, [f(3, atoms)], [VMEM] * 6)(hot, *moved, partial)
    return forces, energy[0]


def solution(mesh):
    both = P(("gx", "gy"))
    in_specs = (
        P(None, ("gx", "gy")),
        both,
        P("gx", "gy", None, None),
        P("gx", "gy", None, None),
        P("gx", "gy"),
    ) + (P(),) * 6
    out_specs = (P(None, ("gx", "gy")), both)
    return jax.shard_map(shards, mesh=mesh, in_specs=in_specs, out_specs=out_specs, check_vma=False)
```

profile of v0, /device:TPU:1, one launch (start us, length us, event | category | flops | bytes accessed | tf_op | source)
XLA Modules:
  0.0 74.9 jit_solution(9628928865288584801)
XLA Ops:
  0.6 1.1 %shard_map.122 = (f32[3,128]{1,0:T(4,128)S(1)}, f32[3,128]{1,0:T(4,128)S(1)}, f32[2,128]{1,0:T(2,128)S(1)}, f32[8,512]{1,0:T(8,128)S(1)}, f32[1,256]{1,0:T(1,128)S(1)}) custom-call(f32[3,512]{1,0:T(4,128)} %pos_in.1, s32[1,512]{1,0:T(1,128)} %bitcast.7, s32[8,32]{1,0:T(8,128)} %bitcast.6), custom_call_target="tpu_custom_call" | custom-call | tf_op jit(solution)/shard_map/pallas_call | solution.py:689
  1.8 2.2 %collective-permute-start.1 = (f32[3,128]{1,0:T(4,128)S(1)}, f32[3,128]{1,0:T(4,128)S(1)}, u32[]{:S(2)}, u32[]{:S(2)}) collective-permute-start(f32[3,128]{1,0:T(4,128)S(1)} %get-tuple-element.192), channel_id=1, source_target_pairs={{0,1},{1,0},{2,3},{3,2},{4,5},{5,4},{6,7},{7,6},{8,9},{9,8},{10,11... | collective-permute-start | bytes 4616 | tf_op jit(solution)/shard_map/ppermute | solution.py:641
  4.0 2.8 %collective-permute-start = (f32[3,128]{1,0:T(4,128)S(1)}, f32[3,128]{1,0:T(4,128)S(1)}, u32[]{:S(2)}, u32[]{:S(2)}) collective-permute-start(f32[3,128]{1,0:T(4,128)S(1)} %get-tuple-element.193), channel_id=1, source_target_pairs={{0,7},{1,2},{2,1},{3,4},{4,3},{5,6},{6,5},{7,0},{8,15},{9,10},{10,... | collective-permute-start | bytes 4616 | tf_op jit(solution)/shard_map/ppermute | solution.py:642
  7.5 2.6 %shard_map.123 = (bf16[256,512]{1,0:T(8,128)(2,1)S(1)}, bf16[256,512]{1,0:T(8,128)(2,1)S(1)}, bf16[2,640,128]{2,1,0:T(8,128)(2,1)S(1)}, bf16[2,8,128]{2,1,0:T(8,...) custom-call(s32[1,1]{1,0:T(1,128)S(6)} %copy.13.count, ...), custom_call_target="tpu_custom_call" | custom-call | tf_op jit(solution)/shard_map/pallas_call | solution.py:700
  10.2 2.8 %collective-permute-start.3 = (f32[3,128]{1,0:T(4,128)S(1)}, f32[3,128]{1,0:T(4,128)S(1)}, u32[]{:S(2)}, u32[]{:S(2)}) collective-permute-start(f32[3,128]{1,0:T(4,128)S(1)} %get-tuple-element.196), channel_id=1, source_target_pairs={{0,248},{8,16},{16,8},{24,32},{32,24},{40,48},{48,40},{56,64},{64,... | collective-permute-start | bytes 4616 | tf_op jit(solution)/shard_map/ppermute | solution.py:642
  13.0 5.5 %collective-permute-start.2 = (f32[3,128]{1,0:T(4,128)S(1)}, f32[3,128]{1,0:T(4,128)S(1)}, u32[]{:S(2)}, u32[]{:S(2)}) collective-permute-start(f32[3,128]{1,0:T(4,128)S(1)} %get-tuple-element.197), channel_id=1, source_target_pairs={{0,8},{8,0},{16,24},{24,16},{32,40},{40,32},{48,56},{56,48},{64,72... | collective-permute-start | bytes 4616 | tf_op jit(solution)/shard_map/ppermute | solution.py:641
  18.4 2.8 %shard_map.124 = (f32[512,256]{1,0:T(8,128)S(1)}, bf16[32,256,256]{2,1,0:T(8,128)(2,1)S(1)}, f32[32,384,128]{2,1,0:T(8,128)S(1)}) custom-call(s32[65]{0:T(128)S(1)} %get-tuple-element.101.plan_own.plan, f32[16,8,128]{2,1,0:T(8,128)S(1)} %get-tuple-element.102.xt, f32[512,8]{1,0:T(8,128)S(1)} %get-tuple-element.100.prc), custom_call_target="tpu_custom_call" | custom-call | tf_op jit(solution)/shard_map/pallas_call | solution.py:715
  21.3 2.0 %shard_map.125 = (f32[512,256]{1,0:T(8,128)S(1)}, f32[8,8,128]{2,1,0:T(8,128)S(1)}, bf16[16,256,256]{2,1,0:T(8,128)(2,1)S(1)}, f32[16,384,128]{2,1,0:T(8,128)S(1...) custom-call(s32[65]{0:T(128)S(1)} %get-tuple-element.95.plan, ...), custom_call_target="tpu_custom_call" | custom-call | tf_op jit(solution)/shard_map/pallas_call | solution.py:718
  23.3 0.1 collective-permute-start.5
  23.4 0.7 collective-permute-start.4
  24.2 2.3 %shard_map.126 = (f32[512,512]{1,0:T(8,128)S(1)}, f32[512,512]{1,0:T(8,128)S(1)}, f32[512,256]{1,0:T(8,128)S(1)}, f32[512,384]{1,0:T(8,128)S(1)}) custom-call(f32[512,256]{1,0:T(8,128)S(1)} %get-tuple-element.110.joined, f32[512,8]{1,0:T(8,128)S(1)} %get-tuple-element.100.prc, bf16[256,512]{1,0:T(8,128)(2,1)S(1)} %get-tuple-element.111.w_hi, ...), custom_call_target="tpu_custom_call" | custom-call | tf_op jit(solution)/shard_map/pallas_call | solution.py:724
  26.5 1.7 %collective-permute-done.5 = f32[96,256]{1,0:T(8,128)S(1)} collective-permute-done((f32[96,256]{1,0:T(8,128)S(1)}, f32[96,256]{1,0:T(8,128)S(1)}, u32[]{:S(2)}, u32[]{:S(2)}) %collective-permute-start.5) | collective-permute-done | bytes 98336 | tf_op jit(solution)/shard_map/ppermute | solution.py:641
  28.2 2.2 %collective-permute-done.4 = f32[96,256]{1,0:T(8,128)S(1)} collective-permute-done((f32[96,256]{1,0:T(8,128)S(1)}, f32[96,256]{1,0:T(8,128)S(1)}, u32[]{:S(2)}, u32[]{:S(2)}) %collective-permute-start.4) | collective-permute-done | bytes 98336 | tf_op jit(solution)/shard_map/ppermute | solution.py:642
  30.5 0.1 collective-permute-start.7
  30.6 2.7 %collective-permute-start.6 = (f32[96,256]{1,0:T(8,128)S(1)}, f32[96,256]{1,0:T(8,128)S(1)}, u32[]{:S(2)}, u32[]{:S(2)}) collective-permute-start(f32[96,256]{1,0:T(8,128)S(1)} %get-tuple-element.165), channel_id=1, source_target_pairs={{0,8},{8,0},{16,24},{24,16},{32,40},{40,32},{48,56},{56,48},{64,72... | collective-permute-start | bytes 294920 | tf_op jit(solution)/shard_map/ppermute | solution.py:641
  33.4 2.9 %shard_map.127.acc_own = f32[512,128]{1,0:T(8,128)S(1)} custom-call(s32[65]{0:T(128)S(1)} %get-tuple-element.101.plan_own.plan, bf16[32,256,256]{2,1,0:T(8,128)(2,1)S(1)} %get-tuple-element.106.tiles, f32[512,512]{1,0:T(8,128)S(1)} %get-tuple-element.122.feat, f32[2,8,128]{2,1,0:T(8,128)S(1)} %get-tuple-element.123.radial), custom_call_target="tpu_custom_call" | custom-call | tf_op jit(solution)/shard_map/pallas_call | solution.py:729
  36.3 6.2 %shard_map.128 = (f32[512,128]{1,0:T(8,128)S(1)}, f32[512,128]{1,0:T(8,128)S(1)}, f32[256,512]{1,0:T(8,128)S(1)}, f32[96,256]{1,0:T(8,128)S(1)}, f32[96,256]{1,0:T(8,128)S(1)}, /*index=5*/f32[64,256]{1,0:T(8,128)S(1)}) custom-call(s32[65]{0:T(128)S(1)} %get-tuple-element.95.plan, bf16[16,256,256]{2,1,0:T(8,128)(2,1)S(1)} %get-tuple-element.107.tiles, ...), custom_call_target="tpu_custom_call" | custom-call | tf_op jit(solution)/shard_map/pallas_call | solution.py:730
  42.6 0.4 collective-permute-start.8
  43.0 2.0 %shard_map.130 = (f32[512,128]{1,0:T(8,128)S(1)}, f32[8,128]{1,0:T(8,128)S(1)}) custom-call(s32[65]{0:T(128)S(1)} %get-tuple-element.95.plan, f32[16,384,128]{2,1,0:T(8,128)S(1)} %get-tuple-element.104.shapes, f32[512,128]{1,0:T(8,128)S(1)} %get-tuple-element.125.grad_acc, f32[2,8,128]{2,1,0:T(8,128)S(1)} %get-tuple-element.123.radial, ...), custom_call_target="tpu_custom_call" | custom-call | tf_op jit(solution)/shard_map/pallas_call | solution.py:744
  45.0 1.1 %collective-permute-done.9 = f32[96,256]{1,0:T(8,128)S(1)} collective-permute-done((f32[96,256]{1,0:T(8,128)S(1)}, f32[96,256]{1,0:T(8,128)S(1)}, u32[]{:S(2)}, u32[]{:S(2)}) %collective-permute-start.9) | collective-permute-done | bytes 98336 | tf_op jit(solution)/shard_map/ppermute | solution.py:641
  46.0 2.2 %collective-permute-done.8 = f32[96,256]{1,0:T(8,128)S(1)} collective-permute-done((f32[96,256]{1,0:T(8,128)S(1)}, f32[96,256]{1,0:T(8,128)S(1)}, u32[]{:S(2)}, u32[]{:S(2)}) %collective-permute-start.8) | collective-permute-done | bytes 98336 | tf_op jit(solution)/shard_map/ppermute | solution.py:642
  48.3 0.4 collective-permute-start.11
  48.7 5.1 %collective-permute-start.10 = (f32[96,256]{1,0:T(8,128)S(1)}, f32[96,256]{1,0:T(8,128)S(1)}, u32[]{:S(2)}, u32[]{:S(2)}) collective-permute-start(f32[96,256]{1,0:T(8,128)S(1)} %get-tuple-element.157), channel_id=1, source_target_pairs={{0,8},{8,0},{16,24},{24,16},{32,40},{40,32},{48,56},{56,48},{64,72... | collective-permute-start | bytes 294920 | tf_op jit(solution)/shard_map/ppermute | solution.py:641
  53.8 5.3 %shard_map.129.quad_own = f32[512,256]{1,0:T(8,128)S(1)} custom-call(s32[65]{0:T(128)S(1)} %get-tuple-element.101.plan_own.plan, bf16[32,256,256]{2,1,0:T(8,128)(2,1)S(1)} %get-tuple-element.106.tiles, f32[512,128]{1,0:T(8,128)S(1)} %get-tuple-element.125.grad_acc, f32[2,8,128]{2,1,0:T(8,128)S(1)} %get-tuple-element.123.radial, ...), custom_call_target="tpu_custom_call" | custom-call | tf_op jit(solution)/shard_map/pallas_call | solution.py:749
  59.1 2.3 %shard_map.131 = (f32[512,256]{1,0:T(8,128)S(1)}, f32[512,128]{1,0:T(8,128)S(1)}, f32[3,128]{1,0:T(4,128)S(1)}, f32[3,128]{1,0:T(4,128)S(1)}, f32[2,128]{1,0:T(2,128)S(1)}) custom-call(s32[65]{0:T(128)S(1)} %get-tuple-element.95.plan, bf16[512,256]{1,0:T(8,128)(2,1)S(1)} %get-tuple-element.94.hot, f32[16,384,128]{2,1,0:T(8,128)S(1)} %get-tuple-element.104.shapes, ...), custom_call_target="tpu_custom_call" | custom-call | tf_op jit(solution)/shard_map/pallas_call | solution.py:752
  61.6 0.6 collective-permute-start.12
  62.2 2.5 %shard_map.132 = (f32[512,128]{1,0:T(8,128)S(1)}, f32[16,128]{1,0:T(8,128)S(1)}, f32[1,512]{1,0:T(1,128)}) custom-call(s32[65]{0:T(128)S(1)} %get-tuple-element.101.plan_own.plan, f32[32,384,128]{2,1,0:T(8,128)S(1)} %get-tuple-element.141.shapes, f32[16,8,128]{2,1,0:T(8,128)S(1)} %get-tuple-element.102.xt, f32[512,256]{1,0:T(8,128)S(1)} %get-tuple-element.142.quad, ...), custom_call_target="tpu_custom_call" | custom-call | tf_op jit(solution)/shard_map/pallas_call | solution.py:760
  64.7 1.5 %collective-permute-done.12 = f32[3,128]{1,0:T(4,128)S(1)} collective-permute-done((f32[3,128]{1,0:T(4,128)S(1)}, f32[3,128]{1,0:T(4,128)S(1)}, u32[]{:S(2)}, u32[]{:S(2)}) %collective-permute-start.12) | collective-permute-done | bytes 1568 | tf_op jit(solution)/shard_map/ppermute | solution.py:642
  66.3 0.1 collective-permute-start.15
  66.4 4.0 %collective-permute-start.14 = (f32[3,128]{1,0:T(4,128)S(1)}, f32[3,128]{1,0:T(4,128)S(1)}, u32[]{:S(2)}, u32[]{:S(2)}) collective-permute-start(f32[3,128]{1,0:T(4,128)S(1)} %get-tuple-element.195), channel_id=1, source_target_pairs={{0,8},{8,0},{16,24},{24,16},{32,40},{40,32},{48,56},{56,48},{64,72... | collective-permute-start | bytes 4616 | tf_op jit(solution)/shard_map/ppermute | solution.py:641
  70.3 3.7 %shard_map.133.partial = f32[3,512]{1,0:T(4,128)S(1)} custom-call(s32[65]{0:T(128)S(1)} %get-tuple-element.101.plan_own.plan, f32[32,384,128]{2,1,0:T(8,128)S(1)} %get-tuple-element.141.shapes, f32[16,8,128]{2,1,0:T(8,128)S(1)} %get-tuple-element.102.xt, f32[512,256]{1,0:T(8,128)S(1)} %get-tuple-element.142.quad, ...), custom_call_target="tpu_custom_call" | custom-call | tf_op jit(solution)/shard_map/pallas_call | solution.py:765
  74.0 0.9 %shard_map.134 = f32[3,512]{1,0:T(4,128)} custom-call(bf16[512,256]{1,0:T(8,128)(2,1)S(1)} %get-tuple-element.94.hot, f32[3,128]{1,0:T(4,128)S(1)} %get-tuple-element.183.left, f32[3,128]{1,0:T(4,128)S(1)} %get-tuple-element.182.right, f32[3,128]{1,0:T(4,128)S(1)} %get-tuple-element.148.up, f32[3,128]{1,0:T(4,128)S(1)} %get-tuple-element.150.down, ...), custom_call_target="tpu_custom_call" | custom-call | tf_op jit(solution)/shard_map/pallas_call | solution.py:771
  (40 shorter events, 0.5 us)
Async XLA Ops:
  1.8 8.3 %collective-permute-start.1 = (f32[3,128]{1,0:T(4,128)S(1)}, f32[3,128]{1,0:T(4,128)S(1)}, u32[]{:S(2)}, u32[]{:S(2)}) collective-permute-start(f32[3,128]{1,0:T(4,128)S(1)} %get-tuple-element.192), channel_id=1, source_target_pairs={{0,1},{1,0},{2,3},{3,2},{4,5},{5,4},{6,7},{7,6},{8,9},{9,8},{10,11... | collective-permute-start | bytes 4616 | tf_op jit(solution)/shard_map/ppermute | solution.py:641
  4.0 6.1 %collective-permute-start = (f32[3,128]{1,0:T(4,128)S(1)}, f32[3,128]{1,0:T(4,128)S(1)}, u32[]{:S(2)}, u32[]{:S(2)}) collective-permute-start(f32[3,128]{1,0:T(4,128)S(1)} %get-tuple-element.193), channel_id=1, source_target_pairs={{0,7},{1,2},{2,1},{3,4},{4,3},{5,6},{6,5},{7,0},{8,15},{9,10},{10,... | collective-permute-start | bytes 4616 | tf_op jit(solution)/shard_map/ppermute | solution.py:642
  10.2 11.1 %collective-permute-start.3 = (f32[3,128]{1,0:T(4,128)S(1)}, f32[3,128]{1,0:T(4,128)S(1)}, u32[]{:S(2)}, u32[]{:S(2)}) collective-permute-start(f32[3,128]{1,0:T(4,128)S(1)} %get-tuple-element.196), channel_id=1, source_target_pairs={{0,248},{8,16},{16,8},{24,32},{32,24},{40,48},{48,40},{56,64},{64,... | collective-permute-start | bytes 4616 | tf_op jit(solution)/shard_map/ppermute | solution.py:642
  13.0 8.3 %collective-permute-start.2 = (f32[3,128]{1,0:T(4,128)S(1)}, f32[3,128]{1,0:T(4,128)S(1)}, u32[]{:S(2)}, u32[]{:S(2)}) collective-permute-start(f32[3,128]{1,0:T(4,128)S(1)} %get-tuple-element.197), channel_id=1, source_target_pairs={{0,8},{8,0},{16,24},{24,16},{32,40},{40,32},{48,56},{56,48},{64,72... | collective-permute-start | bytes 4616 | tf_op jit(solution)/shard_map/ppermute | solution.py:641
  23.3 4.9 %collective-permute-start.5 = (f32[96,256]{1,0:T(8,128)S(1)}, f32[96,256]{1,0:T(8,128)S(1)}, u32[]{:S(2)}, u32[]{:S(2)}) collective-permute-start(f32[96,256]{1,0:T(8,128)S(1)} %get-tuple-element.168), channel_id=1, source_target_pairs={{0,1},{1,0},{2,3},{3,2},{4,5},{5,4},{6,7},{7,6},{8,9},{9,8},{10,11... | collective-permute-start | bytes 294920 | tf_op jit(solution)/shard_map/ppermute | solution.py:641
  23.4 7.0 %collective-permute-start.4 = (f32[96,256]{1,0:T(8,128)S(1)}, f32[96,256]{1,0:T(8,128)S(1)}, u32[]{:S(2)}, u32[]{:S(2)}) collective-permute-start(f32[96,256]{1,0:T(8,128)S(1)} %get-tuple-element.169), channel_id=1, source_target_pairs={{0,7},{1,2},{2,1},{3,4},{4,3},{5,6},{6,5},{7,0},{8,15},{9,10},{10,... | collective-permute-start | bytes 294920 | tf_op jit(solution)/shard_map/ppermute | solution.py:642
  30.5 5.7 %collective-permute-start.7 = (f32[96,256]{1,0:T(8,128)S(1)}, f32[96,256]{1,0:T(8,128)S(1)}, u32[]{:S(2)}, u32[]{:S(2)}) collective-permute-start(f32[96,256]{1,0:T(8,128)S(1)} %get-tuple-element.164), channel_id=1, source_target_pairs={{0,248},{8,16},{16,8},{24,32},{32,24},{40,48},{48,40},{56,64},{64,... | collective-permute-start | bytes 294920 | tf_op jit(solution)/shard_map/ppermute | solution.py:642
  30.6 5.6 %collective-permute-start.6 = (f32[96,256]{1,0:T(8,128)S(1)}, f32[96,256]{1,0:T(8,128)S(1)}, u32[]{:S(2)}, u32[]{:S(2)}) collective-permute-start(f32[96,256]{1,0:T(8,128)S(1)} %get-tuple-element.165), channel_id=1, source_target_pairs={{0,8},{8,0},{16,24},{24,16},{32,40},{40,32},{48,56},{56,48},{64,72... | collective-permute-start | bytes 294920 | tf_op jit(solution)/shard_map/ppermute | solution.py:641
  42.5 3.6 %collective-permute-start.9 = (f32[96,256]{1,0:T(8,128)S(1)}, f32[96,256]{1,0:T(8,128)S(1)}, u32[]{:S(2)}, u32[]{:S(2)}) collective-permute-start(f32[96,256]{1,0:T(8,128)S(1)} %get-tuple-element.160), channel_id=1, source_target_pairs={{0,1},{1,0},{2,3},{3,2},{4,5},{5,4},{6,7},{7,6},{8,9},{9,8},{10,11... | collective-permute-start | bytes 294920 | tf_op jit(solution)/shard_map/ppermute | solution.py:641
  42.6 5.7 %collective-permute-start.8 = (f32[96,256]{1,0:T(8,128)S(1)}, f32[96,256]{1,0:T(8,128)S(1)}, u32[]{:S(2)}, u32[]{:S(2)}) collective-permute-start(f32[96,256]{1,0:T(8,128)S(1)} %get-tuple-element.161), channel_id=1, source_target_pairs={{0,7},{1,2},{2,1},{3,4},{4,3},{5,6},{6,5},{7,0},{8,15},{9,10},{10,... | collective-permute-start | bytes 294920 | tf_op jit(solution)/shard_map/ppermute | solution.py:642
  48.3 10.8 %collective-permute-start.11 = (f32[96,256]{1,0:T(8,128)S(1)}, f32[96,256]{1,0:T(8,128)S(1)}, u32[]{:S(2)}, u32[]{:S(2)}) collective-permute-start(f32[96,256]{1,0:T(8,128)S(1)} %get-tuple-element.156), channel_id=1, source_target_pairs={{0,248},{8,16},{16,8},{24,32},{32,24},{40,48},{48,40},{56,64},{64,... | collective-permute-start | bytes 294920 | tf_op jit(solution)/shard_map/ppermute | solution.py:642
  48.7 10.4 %collective-permute-start.10 = (f32[96,256]{1,0:T(8,128)S(1)}, f32[96,256]{1,0:T(8,128)S(1)}, u32[]{:S(2)}, u32[]{:S(2)}) collective-permute-start(f32[96,256]{1,0:T(8,128)S(1)} %get-tuple-element.157), channel_id=1, source_target_pairs={{0,8},{8,0},{16,24},{24,16},{32,40},{40,32},{48,56},{56,48},{64,72... | collective-permute-start | bytes 294920 | tf_op jit(solution)/shard_map/ppermute | solution.py:641
  61.5 3.2 %collective-permute-start.13 = (f32[3,128]{1,0:T(4,128)S(1)}, f32[3,128]{1,0:T(4,128)S(1)}, u32[]{:S(2)}, u32[]{:S(2)}) collective-permute-start(f32[3,128]{1,0:T(4,128)S(1)} %get-tuple-element.186), channel_id=1, source_target_pairs={{0,1},{1,0},{2,3},{3,2},{4,5},{5,4},{6,7},{7,6},{8,9},{9,8},{10,11... | collective-permute-start | bytes 4616 | tf_op jit(solution)/shard_map/ppermute | solution.py:641
  61.6 4.6 %collective-permute-start.12 = (f32[3,128]{1,0:T(4,128)S(1)}, f32[3,128]{1,0:T(4,128)S(1)}, u32[]{:S(2)}, u32[]{:S(2)}) collective-permute-start(f32[3,128]{1,0:T(4,128)S(1)} %get-tuple-element.187), channel_id=1, source_target_pairs={{0,7},{1,2},{2,1},{3,4},{4,3},{5,6},{6,5},{7,0},{8,15},{9,10},{10,... | collective-permute-start | bytes 4616 | tf_op jit(solution)/shard_map/ppermute | solution.py:642
  66.3 7.7 %collective-permute-start.15 = (f32[3,128]{1,0:T(4,128)S(1)}, f32[3,128]{1,0:T(4,128)S(1)}, u32[]{:S(2)}, u32[]{:S(2)}) collective-permute-start(f32[3,128]{1,0:T(4,128)S(1)} %get-tuple-element.194), channel_id=1, source_target_pairs={{0,248},{8,16},{16,8},{24,32},{32,24},{40,48},{48,40},{56,64},{64,... | collective-permute-start | bytes 4616 | tf_op jit(solution)/shard_map/ppermute | solution.py:642
  66.4 7.6 %collective-permute-start.14 = (f32[3,128]{1,0:T(4,128)S(1)}, f32[3,128]{1,0:T(4,128)S(1)}, u32[]{:S(2)}, u32[]{:S(2)}) collective-permute-start(f32[3,128]{1,0:T(4,128)S(1)} %get-tuple-element.195), channel_id=1, source_target_pairs={{0,8},{8,0},{16,24},{24,16},{32,40},{40,32},{48,56},{56,48},{64,72... | collective-permute-start | bytes 4616 | tf_op jit(solution)/shard_map/ppermute | solution.py:641
where the time goes:
time: 74.7 us; the launch traced here: 74.9 us
  Pallas kernels  36.7 us (49%)
  starting transfers between devices  27.6 us (37%)
  waiting for transfers between devices  8.8 us (12%)
  between operations  1.62 us (2%)
    ppermute x8, starting transfers between devices, swap_both(): one = lax.ppermute(jnp.where(even, to_upper, to_lower), axis, inner)  19.7 us
    ppermute x8, starting transfers between devices, swap_both(): two = lax.ppermute(jnp.where(even, to_lower, to_upper), axis, outer)  7.85 us
    pallas_call x1, Pallas kernels, shards(): call(ghost_second_kernel, [f(atoms, CH), f(atoms, CH), f(ghosts, FEAT)] +...  6.16 us
    ppermute x8, waiting for transfers between devices, swap_both(): two = lax.ppermute(jnp.where(even, to_lower, to_upper), axis, outer)  5.98 us
    pallas_call x1, Pallas kernels, shards(): call(own_grad_kernel, [f(atoms, HIST)], [SMEM] + [VMEM] * 10, [VMEM((atom...  5.33 us
    pallas_call x1, Pallas kernels, shards(): call(own_force_kernel, [f(3, atoms)], [SMEM] + [VMEM] * 8, [VMEM((atoms,...  3.68 us
    pallas_call x1, Pallas kernels, shards(): call(own_second_kernel, [f(atoms, CH)], [SMEM] + [VMEM] * 3)  2.88 us
    pallas_call x1, Pallas kernels, shards(): call(own_first_kernel, [f(atoms, HIST)] + store(SLOTS), [SMEM] + [VMEM] * 2)  2.84 us
  transfers between devices with their start and end apart: 16, of which 5 were waited for; matrix products, arithmetic and copies ran while one was open for 0% of the time, Pallas kernels for 32%

commit v1 on v0

--- a/solution.py
+++ b/solution.py
@@ -488,7 +488,7 @@
         grad_acc[rows, :] = mm3_full(split(gz), mix0, NN)
         return carry
 
-    lax.fori_loop(0, acc.shape[0] // CHUNK, chunk, 0)
+    lax.fori_loop(0, acc.shape[0] // CHUNK, chunk, 0, unroll=True)
 
     def backward(r, c, weight, slot):
         add_feature_grad(r, c, tiles[slot], grad_acc, radial, grad_table)
@@ -565,7 +565,7 @@
         quad[rows, :] = quad_own[rows, :] + (mm(pick, back_hi[...], NN) + mm(pick, back_lo[...], NN))
         return carry
 
-    lax.fori_loop(0, quad.shape[0] // CHUNK, chunk, 0)
+    lax.fori_loop(0, quad.shape[0] // CHUNK, chunk, 0, unroll=True)
 
     def block(r, c, weight, slot):
         add_force(pair_force(first_deriv(r, c, xt, quad), *shape_of(shapes, slot)), r, c, recv, send)

time: 74.7 us -> 72.3 us (0.968)
  Pallas kernels: 36.7 us -> 31.8 us
  starting transfers between devices: 27.6 us -> 30.5 us
  waiting for transfers between devices: 8.8 us -> 7.76 us
    ppermute x8, starting transfers between devices: 19.7 us -> 22.3 us  [swap_both(): one = lax.ppermute(jnp.where(even, to_upper, to_lower), axis, inner)]
    pallas_call x1, Pallas kernels: 6.16 us -> 5.14 us  [shards(): call(ghost_second_kernel, [f(atoms, CH), f(atoms, CH), f(ghosts, FEAT)] +...]
    ppermute x8, waiting for transfers between devices: 2.82 us -> 1.92 us  [swap_both(): one = lax.ppermute(jnp.where(even, to_upper, to_lower), axis, inner)]
    pallas_call x1, Pallas kernels: 2.34 us -> 1.47 us  [shards(): call(ghost_last_kernel, [f(atoms, HIST), f(atoms, LANES)] + three(1, LANE...]
    pallas_call x1, Pallas kernels: 3.68 us -> 2.87 us  [shards(): call(own_force_kernel, [f(3, atoms)], [SMEM] + [VMEM] * 8, [VMEM((atoms,...]
  transfers between devices with their start and end apart: 16 -> 16, of which waited for: 5 -> 5; matrix products, arithmetic and copies ran while one was open for 0% -> 0% of each run, Pallas kernels for 32% -> 30%
where the time goes in v1:
time: 72.3 us; the launch traced here: 72 us
  Pallas kernels  31.8 us (44%)
  starting transfers between devices  30.5 us (42%)
  waiting for transfers between devices  7.76 us (11%)
  between operations  1.65 us (2%)
    ppermute x8, starting transfers between devices, swap_both(): one = lax.ppermute(jnp.where(even, to_upper, to_lower), axis, inner)  22.3 us
    ppermute x8, starting transfers between devices, swap_both(): two = lax.ppermute(jnp.where(even, to_lower, to_upper), axis, outer)  8.13 us
    ppermute x8, waiting for transfers between devices, swap_both(): two = lax.ppermute(jnp.where(even, to_lower, to_upper), axis, outer)  5.84 us
    pallas_call x1, Pallas kernels, shards(): call(ghost_second_kernel, [f(atoms, CH), f(atoms, CH), f(ghosts, FEAT)] +...  5.14 us
    pallas_call x1, Pallas kernels, shards(): call(own_grad_kernel, [f(atoms, HIST)], [SMEM] + [VMEM] * 10, [VMEM((atom...  4.92 us
    pallas_call x1, Pallas kernels, shards(): call(own_force_kernel, [f(3, atoms)], [SMEM] + [VMEM] * 8, [VMEM((atoms,...  2.87 us
    pallas_call x1, Pallas kernels, shards(): call(weight_kernel, [b(HIST, FEAT), b(HIST, FEAT), b(2, 5 * CH, CH), b(2,...  2.56 us
    pallas_call x1, Pallas kernels, shards(): call(own_start_kernel, [f(atoms, LANES), f(OWN, LANES), f(1, atoms)], [SM...  2.48 us
  transfers between devices with their start and end apart: 16, of which 5 were waited for; matrix products, arithmetic and copies ran while one was open for 0% of the time, Pallas kernels for 30%

profile of v1, /device:TPU:1, one launch (start us, length us, event | category | flops | bytes accessed | tf_op | source)
XLA Modules:
  0.0 72.0 jit_solution(4526466428286866394)
XLA Ops:
  0.6 1.1 %shard_map.122 = (f32[3,128]{1,0:T(4,128)S(1)}, f32[3,128]{1,0:T(4,128)S(1)}, f32[2,128]{1,0:T(2,128)S(1)}, f32[8,512]{1,0:T(8,128)S(1)}, f32[1,256]{1,0:T(1,128)S(1)}) custom-call(f32[3,512]{1,0:T(4,128)} %pos_in.1, s32[1,512]{1,0:T(1,128)} %bitcast.7, s32[8,32]{1,0:T(8,128)} %bitcast.6), custom_call_target="tpu_custom_call" | custom-call | tf_op jit(solution)/shard_map/pallas_call | solution.py:689
  1.8 2.2 %collective-permute-start.1 = (f32[3,128]{1,0:T(4,128)S(1)}, f32[3,128]{1,0:T(4,128)S(1)}, u32[]{:S(2)}, u32[]{:S(2)}) collective-permute-start(f32[3,128]{1,0:T(4,128)S(1)} %get-tuple-element.192), channel_id=1, source_target_pairs={{0,1},{1,0},{2,3},{3,2},{4,5},{5,4},{6,7},{7,6},{8,9},{9,8},{10,11... | collective-permute-start | bytes 4616 | tf_op jit(solution)/shard_map/ppermute | solution.py:641
  4.0 2.8 %collective-permute-start = (f32[3,128]{1,0:T(4,128)S(1)}, f32[3,128]{1,0:T(4,128)S(1)}, u32[]{:S(2)}, u32[]{:S(2)}) collective-permute-start(f32[3,128]{1,0:T(4,128)S(1)} %get-tuple-element.193), channel_id=1, source_target_pairs={{0,7},{1,2},{2,1},{3,4},{4,3},{5,6},{6,5},{7,0},{8,15},{9,10},{10,... | collective-permute-start | bytes 4616 | tf_op jit(solution)/shard_map/ppermute | solution.py:642
  7.5 2.6 %shard_map.123 = (bf16[256,512]{1,0:T(8,128)(2,1)S(1)}, bf16[256,512]{1,0:T(8,128)(2,1)S(1)}, bf16[2,640,128]{2,1,0:T(8,128)(2,1)S(1)}, bf16[2,8,128]{2,1,0:T(8,...) custom-call(s32[1,1]{1,0:T(1,128)S(6)} %copy.13.count, ...), custom_call_target="tpu_custom_call" | custom-call | tf_op jit(solution)/shard_map/pallas_call | solution.py:700
  10.1 2.9 %collective-permute-start.3 = (f32[3,128]{1,0:T(4,128)S(1)}, f32[3,128]{1,0:T(4,128)S(1)}, u32[]{:S(2)}, u32[]{:S(2)}) collective-permute-start(f32[3,128]{1,0:T(4,128)S(1)} %get-tuple-element.196), channel_id=1, source_target_pairs={{0,248},{8,16},{16,8},{24,32},{32,24},{40,48},{48,40},{56,64},{64,... | collective-permute-start | bytes 4616 | tf_op jit(solution)/shard_map/ppermute | solution.py:642
  13.0 5.4 %collective-permute-start.2 = (f32[3,128]{1,0:T(4,128)S(1)}, f32[3,128]{1,0:T(4,128)S(1)}, u32[]{:S(2)}, u32[]{:S(2)}) collective-permute-start(f32[3,128]{1,0:T(4,128)S(1)} %get-tuple-element.197), channel_id=1, source_target_pairs={{0,8},{8,0},{16,24},{24,16},{32,40},{40,32},{48,56},{56,48},{64,72... | collective-permute-start | bytes 4616 | tf_op jit(solution)/shard_map/ppermute | solution.py:641
  18.4 2.4 %shard_map.124 = (f32[512,256]{1,0:T(8,128)S(1)}, bf16[32,256,256]{2,1,0:T(8,128)(2,1)S(1)}, f32[32,384,128]{2,1,0:T(8,128)S(1)}) custom-call(s32[65]{0:T(128)S(1)} %get-tuple-element.101.plan_own.plan, f32[16,8,128]{2,1,0:T(8,128)S(1)} %get-tuple-element.102.xt, f32[512,8]{1,0:T(8,128)S(1)} %get-tuple-element.100.prc), custom_call_target="tpu_custom_call" | custom-call | tf_op jit(solution)/shard_map/pallas_call | solution.py:715
  20.8 1.7 %shard_map.125 = (f32[512,256]{1,0:T(8,128)S(1)}, f32[8,8,128]{2,1,0:T(8,128)S(1)}, bf16[16,256,256]{2,1,0:T(8,128)(2,1)S(1)}, f32[16,384,128]{2,1,0:T(8,128)S(1...) custom-call(s32[65]{0:T(128)S(1)} %get-tuple-element.95.plan, ...), custom_call_target="tpu_custom_call" | custom-call | tf_op jit(solution)/shard_map/pallas_call | solution.py:718
  22.5 0.1 collective-permute-start.5
  22.6 1.1 %collective-permute-start.4 = (f32[96,256]{1,0:T(8,128)S(1)}, f32[96,256]{1,0:T(8,128)S(1)}, u32[]{:S(2)}, u32[]{:S(2)}) collective-permute-start(f32[96,256]{1,0:T(8,128)S(1)} %get-tuple-element.169), channel_id=1, source_target_pairs={{0,7},{1,2},{2,1},{3,4},{4,3},{5,6},{6,5},{7,0},{8,15},{9,10},{10,... | collective-permute-start | bytes 294920 | tf_op jit(solution)/shard_map/ppermute | solution.py:642
  23.7 2.3 %shard_map.126 = (f32[512,512]{1,0:T(8,128)S(1)}, f32[512,512]{1,0:T(8,128)S(1)}, f32[512,256]{1,0:T(8,128)S(1)}, f32[512,384]{1,0:T(8,128)S(1)}) custom-call(f32[512,256]{1,0:T(8,128)S(1)} %get-tuple-element.110.joined, f32[512,8]{1,0:T(8,128)S(1)} %get-tuple-element.100.prc, bf16[256,512]{1,0:T(8,128)(2,1)S(1)} %get-tuple-element.111.w_hi, ...), custom_call_target="tpu_custom_call" | custom-call | tf_op jit(solution)/shard_map/pallas_call | solution.py:724
  26.0 1.0 %collective-permute-done.5 = f32[96,256]{1,0:T(8,128)S(1)} collective-permute-done((f32[96,256]{1,0:T(8,128)S(1)}, f32[96,256]{1,0:T(8,128)S(1)}, u32[]{:S(2)}, u32[]{:S(2)}) %collective-permute-start.5) | collective-permute-done | bytes 98336 | tf_op jit(solution)/shard_map/ppermute | solution.py:641
  27.0 1.6 %collective-permute-done.4 = f32[96,256]{1,0:T(8,128)S(1)} collective-permute-done((f32[96,256]{1,0:T(8,128)S(1)}, f32[96,256]{1,0:T(8,128)S(1)}, u32[]{:S(2)}, u32[]{:S(2)}) %collective-permute-start.4) | collective-permute-done | bytes 98336 | tf_op jit(solution)/shard_map/ppermute | solution.py:642
  28.7 0.1 collective-permute-start.7
  28.8 4.5 %collective-permute-start.6 = (f32[96,256]{1,0:T(8,128)S(1)}, f32[96,256]{1,0:T(8,128)S(1)}, u32[]{:S(2)}, u32[]{:S(2)}) collective-permute-start(f32[96,256]{1,0:T(8,128)S(1)} %get-tuple-element.165), channel_id=1, source_target_pairs={{0,8},{8,0},{16,24},{24,16},{32,40},{40,32},{48,56},{56,48},{64,72... | collective-permute-start | bytes 294920 | tf_op jit(solution)/shard_map/ppermute | solution.py:641
  33.3 2.4 %shard_map.127.acc_own = f32[512,128]{1,0:T(8,128)S(1)} custom-call(s32[65]{0:T(128)S(1)} %get-tuple-element.101.plan_own.plan, bf16[32,256,256]{2,1,0:T(8,128)(2,1)S(1)} %get-tuple-element.106.tiles, f32[512,512]{1,0:T(8,128)S(1)} %get-tuple-element.122.feat, f32[2,8,128]{2,1,0:T(8,128)S(1)} %get-tuple-element.123.radial), custom_call_target="tpu_custom_call" | custom-call | tf_op jit(solution)/shard_map/pallas_call | solution.py:729
  35.8 5.1 %shard_map.128 = (f32[512,128]{1,0:T(8,128)S(1)}, f32[512,128]{1,0:T(8,128)S(1)}, f32[256,512]{1,0:T(8,128)S(1)}, f32[96,256]{1,0:T(8,128)S(1)}, f32[96,256]{1,0:T(8,128)S(1)}, /*index=5*/f32[64,256]{1,0:T(8,128)S(1)}) custom-call(s32[65]{0:T(128)S(1)} %get-tuple-element.95.plan, bf16[16,256,256]{2,1,0:T(8,128)(2,1)S(1)} %get-tuple-element.107.tiles, ...), custom_call_target="tpu_custom_call" | custom-call | tf_op jit(solution)/shard_map/pallas_call | solution.py:730
  41.1 1.0 %collective-permute-start.8 = (f32[96,256]{1,0:T(8,128)S(1)}, f32[96,256]{1,0:T(8,128)S(1)}, u32[]{:S(2)}, u32[]{:S(2)}) collective-permute-start(f32[96,256]{1,0:T(8,128)S(1)} %get-tuple-element.161), channel_id=1, source_target_pairs={{0,7},{1,2},{2,1},{3,4},{4,3},{5,6},{6,5},{7,0},{8,15},{9,10},{10,... | collective-permute-start | bytes 294920 | tf_op jit(solution)/shard_map/ppermute | solution.py:642
  42.1 1.5 %shard_map.130 = (f32[512,128]{1,0:T(8,128)S(1)}, f32[8,128]{1,0:T(8,128)S(1)}) custom-call(s32[65]{0:T(128)S(1)} %get-tuple-element.95.plan, f32[16,384,128]{2,1,0:T(8,128)S(1)} %get-tuple-element.104.shapes, f32[512,128]{1,0:T(8,128)S(1)} %get-tuple-element.125.grad_acc, f32[2,8,128]{2,1,0:T(8,128)S(1)} %get-tuple-element.123.radial, ...), custom_call_target="tpu_custom_call" | custom-call | tf_op jit(solution)/shard_map/pallas_call | solution.py:744
  43.6 0.9 %collective-permute-done.9 = f32[96,256]{1,0:T(8,128)S(1)} collective-permute-done((f32[96,256]{1,0:T(8,128)S(1)}, f32[96,256]{1,0:T(8,128)S(1)}, u32[]{:S(2)}, u32[]{:S(2)}) %collective-permute-start.9) | collective-permute-done | bytes 98336 | tf_op jit(solution)/shard_map/ppermute | solution.py:641
  44.5 2.2 %collective-permute-done.8 = f32[96,256]{1,0:T(8,128)S(1)} collective-permute-done((f32[96,256]{1,0:T(8,128)S(1)}, f32[96,256]{1,0:T(8,128)S(1)}, u32[]{:S(2)}, u32[]{:S(2)}) %collective-permute-start.8) | collective-permute-done | bytes 98336 | tf_op jit(solution)/shard_map/ppermute | solution.py:642
  46.8 0.1 collective-permute-start.11
  46.9 6.3 %collective-permute-start.10 = (f32[96,256]{1,0:T(8,128)S(1)}, f32[96,256]{1,0:T(8,128)S(1)}, u32[]{:S(2)}, u32[]{:S(2)}) collective-permute-start(f32[96,256]{1,0:T(8,128)S(1)} %get-tuple-element.157), channel_id=1, source_target_pairs={{0,8},{8,0},{16,24},{24,16},{32,40},{40,32},{48,56},{56,48},{64,72... | collective-permute-start | bytes 294920 | tf_op jit(solution)/shard_map/ppermute | solution.py:641
  53.3 4.9 %shard_map.129.quad_own = f32[512,256]{1,0:T(8,128)S(1)} custom-call(s32[65]{0:T(128)S(1)} %get-tuple-element.101.plan_own.plan, bf16[32,256,256]{2,1,0:T(8,128)(2,1)S(1)} %get-tuple-element.106.tiles, f32[512,128]{1,0:T(8,128)S(1)} %get-tuple-element.125.grad_acc, f32[2,8,128]{2,1,0:T(8,128)S(1)} %get-tuple-element.123.radial, ...), custom_call_target="tpu_custom_call" | custom-call | tf_op jit(solution)/shard_map/pallas_call | solution.py:749
  58.2 1.5 %shard_map.131 = (f32[512,256]{1,0:T(8,128)S(1)}, f32[512,128]{1,0:T(8,128)S(1)}, f32[3,128]{1,0:T(4,128)S(1)}, f32[3,128]{1,0:T(4,128)S(1)}, f32[2,128]{1,0:T(2,128)S(1)}) custom-call(s32[65]{0:T(128)S(1)} %get-tuple-element.95.plan, bf16[512,256]{1,0:T(8,128)(2,1)S(1)} %get-tuple-element.94.hot, f32[16,384,128]{2,1,0:T(8,128)S(1)} %get-tuple-element.104.shapes, ...), custom_call_target="tpu_custom_call" | custom-call | tf_op jit(solution)/shard_map/pallas_call | solution.py:752
  59.8 0.1 collective-permute-start.12
  59.9 2.5 %shard_map.132 = (f32[512,128]{1,0:T(8,128)S(1)}, f32[16,128]{1,0:T(8,128)S(1)}, f32[1,512]{1,0:T(1,128)}) custom-call(s32[65]{0:T(128)S(1)} %get-tuple-element.101.plan_own.plan, f32[32,384,128]{2,1,0:T(8,128)S(1)} %get-tuple-element.141.shapes, f32[16,8,128]{2,1,0:T(8,128)S(1)} %get-tuple-element.102.xt, f32[512,256]{1,0:T(8,128)S(1)} %get-tuple-element.142.quad, ...), custom_call_target="tpu_custom_call" | custom-call | tf_op jit(solution)/shard_map/pallas_call | solution.py:760
  62.4 2.0 %collective-permute-done.12 = f32[3,128]{1,0:T(4,128)S(1)} collective-permute-done((f32[3,128]{1,0:T(4,128)S(1)}, f32[3,128]{1,0:T(4,128)S(1)}, u32[]{:S(2)}, u32[]{:S(2)}) %collective-permute-start.12) | collective-permute-done | bytes 1568 | tf_op jit(solution)/shard_map/ppermute | solution.py:642
  64.5 0.1 collective-permute-start.15
  64.6 3.6 %collective-permute-start.14 = (f32[3,128]{1,0:T(4,128)S(1)}, f32[3,128]{1,0:T(4,128)S(1)}, u32[]{:S(2)}, u32[]{:S(2)}) collective-permute-start(f32[3,128]{1,0:T(4,128)S(1)} %get-tuple-element.195), channel_id=1, source_target_pairs={{0,8},{8,0},{16,24},{24,16},{32,40},{40,32},{48,56},{56,48},{64,72... | collective-permute-start | bytes 4616 | tf_op jit(solution)/shard_map/ppermute | solution.py:641
  68.2 2.9 %shard_map.133.partial = f32[3,512]{1,0:T(4,128)S(1)} custom-call(s32[65]{0:T(128)S(1)} %get-tuple-element.101.plan_own.plan, f32[32,384,128]{2,1,0:T(8,128)S(1)} %get-tuple-element.141.shapes, f32[16,8,128]{2,1,0:T(8,128)S(1)} %get-tuple-element.102.xt, f32[512,256]{1,0:T(8,128)S(1)} %get-tuple-element.142.quad, ...), custom_call_target="tpu_custom_call" | custom-call | tf_op jit(solution)/shard_map/pallas_call | solution.py:765
  71.1 0.9 %shard_map.134 = f32[3,512]{1,0:T(4,128)} custom-call(bf16[512,256]{1,0:T(8,128)(2,1)S(1)} %get-tuple-element.94.hot, f32[3,128]{1,0:T(4,128)S(1)} %get-tuple-element.183.left, f32[3,128]{1,0:T(4,128)S(1)} %get-tuple-element.182.right, f32[3,128]{1,0:T(4,128)S(1)} %get-tuple-element.148.up, f32[3,128]{1,0:T(4,128)S(1)} %get-tuple-element.150.down, ...), custom_call_target="tpu_custom_call" | custom-call | tf_op jit(solution)/shard_map/pallas_call | solution.py:771
  (40 shorter events, 0.5 us)
Async XLA Ops:
  1.8 8.3 %collective-permute-start.1 = (f32[3,128]{1,0:T(4,128)S(1)}, f32[3,128]{1,0:T(4,128)S(1)}, u32[]{:S(2)}, u32[]{:S(2)}) collective-permute-start(f32[3,128]{1,0:T(4,128)S(1)} %get-tuple-element.192), channel_id=1, source_target_pairs={{0,1},{1,0},{2,3},{3,2},{4,5},{5,4},{6,7},{7,6},{8,9},{9,8},{10,11... | collective-permute-start | bytes 4616 | tf_op jit(solution)/shard_map/ppermute | solution.py:641
  4.0 6.1 %collective-permute-start = (f32[3,128]{1,0:T(4,128)S(1)}, f32[3,128]{1,0:T(4,128)S(1)}, u32[]{:S(2)}, u32[]{:S(2)}) collective-permute-start(f32[3,128]{1,0:T(4,128)S(1)} %get-tuple-element.193), channel_id=1, source_target_pairs={{0,7},{1,2},{2,1},{3,4},{4,3},{5,6},{6,5},{7,0},{8,15},{9,10},{10,... | collective-permute-start | bytes 4616 | tf_op jit(solution)/shard_map/ppermute | solution.py:642
  10.1 10.7 %collective-permute-start.3 = (f32[3,128]{1,0:T(4,128)S(1)}, f32[3,128]{1,0:T(4,128)S(1)}, u32[]{:S(2)}, u32[]{:S(2)}) collective-permute-start(f32[3,128]{1,0:T(4,128)S(1)} %get-tuple-element.196), channel_id=1, source_target_pairs={{0,248},{8,16},{16,8},{24,32},{32,24},{40,48},{48,40},{56,64},{64,... | collective-permute-start | bytes 4616 | tf_op jit(solution)/shard_map/ppermute | solution.py:642
  13.0 7.8 %collective-permute-start.2 = (f32[3,128]{1,0:T(4,128)S(1)}, f32[3,128]{1,0:T(4,128)S(1)}, u32[]{:S(2)}, u32[]{:S(2)}) collective-permute-start(f32[3,128]{1,0:T(4,128)S(1)} %get-tuple-element.197), channel_id=1, source_target_pairs={{0,8},{8,0},{16,24},{24,16},{32,40},{40,32},{48,56},{56,48},{64,72... | collective-permute-start | bytes 4616 | tf_op jit(solution)/shard_map/ppermute | solution.py:641
  22.5 4.5 %collective-permute-start.5 = (f32[96,256]{1,0:T(8,128)S(1)}, f32[96,256]{1,0:T(8,128)S(1)}, u32[]{:S(2)}, u32[]{:S(2)}) collective-permute-start(f32[96,256]{1,0:T(8,128)S(1)} %get-tuple-element.168), channel_id=1, source_target_pairs={{0,1},{1,0},{2,3},{3,2},{4,5},{5,4},{6,7},{7,6},{8,9},{9,8},{10,11... | collective-permute-start | bytes 294920 | tf_op jit(solution)/shard_map/ppermute | solution.py:641
  22.6 6.0 %collective-permute-start.4 = (f32[96,256]{1,0:T(8,128)S(1)}, f32[96,256]{1,0:T(8,128)S(1)}, u32[]{:S(2)}, u32[]{:S(2)}) collective-permute-start(f32[96,256]{1,0:T(8,128)S(1)} %get-tuple-element.169), channel_id=1, source_target_pairs={{0,7},{1,2},{2,1},{3,4},{4,3},{5,6},{6,5},{7,0},{8,15},{9,10},{10,... | collective-permute-start | bytes 294920 | tf_op jit(solution)/shard_map/ppermute | solution.py:642
  28.7 7.1 %collective-permute-start.7 = (f32[96,256]{1,0:T(8,128)S(1)}, f32[96,256]{1,0:T(8,128)S(1)}, u32[]{:S(2)}, u32[]{:S(2)}) collective-permute-start(f32[96,256]{1,0:T(8,128)S(1)} %get-tuple-element.164), channel_id=1, source_target_pairs={{0,248},{8,16},{16,8},{24,32},{32,24},{40,48},{48,40},{56,64},{64,... | collective-permute-start | bytes 294920 | tf_op jit(solution)/shard_map/ppermute | solution.py:642
  28.8 7.0 %collective-permute-start.6 = (f32[96,256]{1,0:T(8,128)S(1)}, f32[96,256]{1,0:T(8,128)S(1)}, u32[]{:S(2)}, u32[]{:S(2)}) collective-permute-start(f32[96,256]{1,0:T(8,128)S(1)} %get-tuple-element.165), channel_id=1, source_target_pairs={{0,8},{8,0},{16,24},{24,16},{32,40},{40,32},{48,56},{56,48},{64,72... | collective-permute-start | bytes 294920 | tf_op jit(solution)/shard_map/ppermute | solution.py:641
  41.0 3.6 %collective-permute-start.9 = (f32[96,256]{1,0:T(8,128)S(1)}, f32[96,256]{1,0:T(8,128)S(1)}, u32[]{:S(2)}, u32[]{:S(2)}) collective-permute-start(f32[96,256]{1,0:T(8,128)S(1)} %get-tuple-element.160), channel_id=1, source_target_pairs={{0,1},{1,0},{2,3},{3,2},{4,5},{5,4},{6,7},{7,6},{8,9},{9,8},{10,11... | collective-permute-start | bytes 294920 | tf_op jit(solution)/shard_map/ppermute | solution.py:641
  41.1 5.7 %collective-permute-start.8 = (f32[96,256]{1,0:T(8,128)S(1)}, f32[96,256]{1,0:T(8,128)S(1)}, u32[]{:S(2)}, u32[]{:S(2)}) collective-permute-start(f32[96,256]{1,0:T(8,128)S(1)} %get-tuple-element.161), channel_id=1, source_target_pairs={{0,7},{1,2},{2,1},{3,4},{4,3},{5,6},{6,5},{7,0},{8,15},{9,10},{10,... | collective-permute-start | bytes 294920 | tf_op jit(solution)/shard_map/ppermute | solution.py:642
  46.8 11.4 %collective-permute-start.11 = (f32[96,256]{1,0:T(8,128)S(1)}, f32[96,256]{1,0:T(8,128)S(1)}, u32[]{:S(2)}, u32[]{:S(2)}) collective-permute-start(f32[96,256]{1,0:T(8,128)S(1)} %get-tuple-element.156), channel_id=1, source_target_pairs={{0,248},{8,16},{16,8},{24,32},{32,24},{40,48},{48,40},{56,64},{64,... | collective-permute-start | bytes 294920 | tf_op jit(solution)/shard_map/ppermute | solution.py:642
  46.9 11.3 %collective-permute-start.10 = (f32[96,256]{1,0:T(8,128)S(1)}, f32[96,256]{1,0:T(8,128)S(1)}, u32[]{:S(2)}, u32[]{:S(2)}) collective-permute-start(f32[96,256]{1,0:T(8,128)S(1)} %get-tuple-element.157), channel_id=1, source_target_pairs={{0,8},{8,0},{16,24},{24,16},{32,40},{40,32},{48,56},{56,48},{64,72... | collective-permute-start | bytes 294920 | tf_op jit(solution)/shard_map/ppermute | solution.py:641
  59.7 2.7 %collective-permute-start.13 = (f32[3,128]{1,0:T(4,128)S(1)}, f32[3,128]{1,0:T(4,128)S(1)}, u32[]{:S(2)}, u32[]{:S(2)}) collective-permute-start(f32[3,128]{1,0:T(4,128)S(1)} %get-tuple-element.186), channel_id=1, source_target_pairs={{0,1},{1,0},{2,3},{3,2},{4,5},{5,4},{6,7},{7,6},{8,9},{9,8},{10,11... | collective-permute-start | bytes 4616 | tf_op jit(solution)/shard_map/ppermute | solution.py:641
  59.8 4.6 %collective-permute-start.12 = (f32[3,128]{1,0:T(4,128)S(1)}, f32[3,128]{1,0:T(4,128)S(1)}, u32[]{:S(2)}, u32[]{:S(2)}) collective-permute-start(f32[3,128]{1,0:T(4,128)S(1)} %get-tuple-element.187), channel_id=1, source_target_pairs={{0,7},{1,2},{2,1},{3,4},{4,3},{5,6},{6,5},{7,0},{8,15},{9,10},{10,... | collective-permute-start | bytes 4616 | tf_op jit(solution)/shard_map/ppermute | solution.py:642
  64.5 6.6 %collective-permute-start.15 = (f32[3,128]{1,0:T(4,128)S(1)}, f32[3,128]{1,0:T(4,128)S(1)}, u32[]{:S(2)}, u32[]{:S(2)}) collective-permute-start(f32[3,128]{1,0:T(4,128)S(1)} %get-tuple-element.194), channel_id=1, source_target_pairs={{0,248},{8,16},{16,8},{24,32},{32,24},{40,48},{48,40},{56,64},{64,... | collective-permute-start | bytes 4616 | tf_op jit(solution)/shard_map/ppermute | solution.py:642
  64.6 6.5 %collective-permute-start.14 = (f32[3,128]{1,0:T(4,128)S(1)}, f32[3,128]{1,0:T(4,128)S(1)}, u32[]{:S(2)}, u32[]{:S(2)}) collective-permute-start(f32[3,128]{1,0:T(4,128)S(1)} %get-tuple-element.195), channel_id=1, source_target_pairs={{0,8},{8,0},{16,24},{24,16},{32,40},{40,32},{48,56},{56,48},{64,72... | collective-permute-start | bytes 4616 | tf_op jit(solution)/shard_map/ppermute | solution.py:641
